TPU v7x, 32 devices: a whole 2x2x4 slice. The times are simulated.
32 devices in a mesh: expert: 16 (over z, y, x), pair: 2 (over core).
Axes of the slice: x: 2, y: 2, z: 4, core: 2. Of those that a mesh axis runs over, the one named last changes fastest.
Arguments:
- tokens: bfloat16 [192, 196, 1024], P(('expert', 'pair')), may hold values from -64 to 64
- router: bfloat16 [1024, 16], replicated, as said below
- w_in: bfloat16 [16, 1024, 4096], P('expert', None, 'pair'), may hold values from -0.1875 to 0.1875
- w_out: bfloat16 [16, 4096, 1024], P('expert', 'pair'), may hold values from -0.09375 to 0.09375
- out_grad: bfloat16 [192, 196, 1024], P(('expert', 'pair')), may hold values from -6 to 6
Outputs:
- tokens_grad: bfloat16 [192, 196, 1024], P(('expert', 'pair'))
- w_in_grad: bfloat16 [16, 1024, 4096], P('expert', None, 'pair')
- w_out_grad: bfloat16 [16, 4096, 1024], P('expert', 'pair')
- router_grad: float32 [1024, 16], replicated
Inputs may be any that keep to these rules, and one draw needn't show every extreme that they name: `router`: entries are normal with deviation 1024 ** -0.5, cut at five deviations.
All inputs are finite; a program needn't handle non-finite values.
Results may differ from a plain program's by a relative error of at most 0.0087.
Values may be sent and summed in bfloat16 or wider, within the bound.
No kernel may reach another device: no remote copies, remote signals or barrier semaphores. Data moves between devices by JAX's collectives and lax.ppermute only.
A program may use at most 128 MiB of HBM per device.

v0:
```python
import jax
import jax.numpy as jnp
from jax import lax
from jax.sharding import PartitionSpec as P


def per_device(tokens, router, w_in, w_out, out_grad):
    local_count, tok_count, width = tokens.shape
    expert_count = router.shape[1]
    flat_tokens = tokens.reshape(local_count * tok_count, width)
    logits = jnp.dot(flat_tokens, router, preferred_element_type=jnp.float32)
    logits = logits.reshape(local_count, tok_count, expert_count)
    dispatch = jax.nn.softmax(logits, axis=1)
    combine = jax.nn.softmax(logits, axis=2)
    dispatch_b = dispatch.astype(jnp.bfloat16)
    combine_b = combine.astype(jnp.bfloat16)
    slot_values = jnp.einsum(
        "nme,nmd->ned", dispatch_b, tokens, preferred_element_type=jnp.float32
    ).astype(jnp.bfloat16)
    slot_cot = jnp.einsum(
        "nme,nmd->ned", combine_b, out_grad, preferred_element_type=jnp.float32
    ).astype(jnp.bfloat16)
    moved = (
        lax.all_to_all(slot_values, "expert", split_axis=1, concat_axis=0, tiled=True),
        lax.all_to_all(slot_cot, "expert", split_axis=1, concat_axis=0, tiled=True),
    )
    slot_rows, cot_rows = (
        lax.all_gather(moved[0], "pair", axis=0, tiled=True),
        lax.all_gather(moved[1], "pair", axis=0, tiled=True),
    )
    slot_rows = slot_rows[:, 0, :]
    cot_rows = cot_rows[:, 0, :]
    weight_in = w_in[0]
    weight_out = w_out[0]
    hidden = jnp.dot(slot_rows, weight_in, preferred_element_type=jnp.float32)
    activated = jax.nn.gelu(hidden).astype(jnp.bfloat16)
    out_partial = jnp.dot(activated, weight_out, preferred_element_type=jnp.float32)
    act_grad = lax.dot_general(
        cot_rows, weight_out, (((1,), (1,)), ((), ())), preferred_element_type=jnp.float32
    )
    unused, pullback = jax.vjp(jax.nn.gelu, hidden)
    hidden_grad = pullback(act_grad)[0].astype(jnp.bfloat16)
    grad_partial = lax.dot_general(
        hidden_grad, weight_in, (((1,), (1,)), ((), ())), preferred_element_type=jnp.float32
    )
    grad_in = lax.dot_general(
        slot_rows, hidden_grad, (((0,), (0,)), ((), ())), preferred_element_type=jnp.float32
    )
    grad_out = lax.dot_general(
        activated, cot_rows, (((0,), (0,)), ((), ())), preferred_element_type=jnp.float32
    )
    out_summed, grad_summed = (
        lax.psum_scatter(out_partial, "pair", scatter_dimension=0, tiled=True),
        lax.psum_scatter(grad_partial, "pair", scatter_dimension=0, tiled=True),
    )
    out_rows = out_summed.astype(jnp.bfloat16)[:, None, :]
    grad_rows = grad_summed.astype(jnp.bfloat16)[:, None, :]
    expert_out, slot_grad = (
        lax.all_to_all(out_rows, "expert", split_axis=0, concat_axis=1, tiled=True),
        lax.all_to_all(grad_rows, "expert", split_axis=0, concat_axis=1, tiled=True),
    )
    comb_cot = jnp.einsum("nmd,ned->nme", out_grad, expert_out, preferred_element_type=jnp.float32)
    comb_logit = combine * (comb_cot - jnp.sum(combine * comb_cot, axis=2, keepdims=True))
    disp_cot = jnp.einsum("nmd,ned->nme", tokens, slot_grad, preferred_element_type=jnp.float32)
    disp_logit = dispatch * (disp_cot - jnp.sum(dispatch * disp_cot, axis=1, keepdims=True))
    logit_grad = (comb_logit + disp_logit).astype(jnp.bfloat16)
    flat_logit = logit_grad.reshape(local_count * tok_count, expert_count)
    through_slots = jnp.einsum(
        "nme,ned->nmd", dispatch_b, slot_grad, preferred_element_type=jnp.float32
    )
    through_logits = lax.dot_general(
        flat_logit, router, (((1,), (1,)), ((), ())), preferred_element_type=jnp.float32
    )
    tokens_grad = (through_slots + through_logits.reshape(local_count, tok_count, width)).astype(
        jnp.bfloat16
    )
    router_part = lax.dot_general(
        flat_tokens, flat_logit, (((0,), (0,)), ((), ())), preferred_element_type=jnp.float32
    )
    router_grad = lax.psum(router_part, ("expert", "pair"))
    return (
        tokens_grad,
        grad_in.astype(jnp.bfloat16)[None],
        grad_out.astype(jnp.bfloat16)[None],
        router_grad,
    )


def solution(mesh):
    in_specs = (
        P(("expert", "pair"), None, None),
        P(),
        P("expert", None, "pair"),
        P("expert", "pair", None),
        P(("expert", "pair"), None, None),
    )
    out_specs = (
        P(("expert", "pair"), None, None),
        P("expert", None, "pair"),
        P("expert", "pair", None),
        P(),
    )
    return jax.shard_map(
        per_device, mesh=mesh, in_specs=in_specs, out_specs=out_specs, check_vma=False
    )
```

profile of v0, /device:TPU:1, one launch (start us, length us, event | category | flops | bytes accessed | tf_op | source)
XLA Modules:
  0.0 226.6 jit_solution(12008124195808510058)
XLA Ops:
  7.2 1.7 copy-done
  8.9 1.5 fusion.49
  10.4 1.0 fusion.55
  11.4 0.6 convolution_convert_fusion
  11.9 0.8 copy.16
  12.8 7.4 %all-to-all-start.1 = ((bf16[6,16,1024]{2,0,1:T(8,128)(2,1)}), bf16[6,16,1024]{2,0,1:T(8,128)(2,1)S(1)}, u32[]{:S(2)}, u32[]{:S(2)}) async-start(bf16[6,16,1024]{2,0,1:T(8,128)(2,1)} %copy.16), calls=%async_computation.1 | async-start | bytes 524288 | tf_op jit(solution)/shard_map/all_to_all | solution.py:24
  20.2 0.7 fusion.56
  20.8 2.2 convolution_convert_fusion.1
  23.1 0.8 copy.15
  23.9 4.3 %all-to-all-done.1 = bf16[6,16,1024]{2,0,1:T(8,128)(2,1)S(1)} async-done(((bf16[6,16,1024]{2,0,1:T(8,128)(2,1)}), bf16[6,16,1024]{2,0,1:T(8,128)(2,1)S(1)}, u32[]{:S(2)}, u32[]{:S(2)}) %all-to-all-start.1) | async-done | bytes 196640 | tf_op jit(solution)/shard_map/all_to_all | solution.py:24
  28.2 4.8 %all-to-all-start = ((bf16[6,16,1024]{2,0,1:T(8,128)(2,1)}), bf16[6,16,1024]{2,0,1:T(8,128)(2,1)S(1)}, u32[]{:S(2)}, u32[]{:S(2)}) async-start(bf16[6,16,1024]{2,0,1:T(8,128)(2,1)} %copy.15), calls=%async_computation | async-start | bytes 524288 | tf_op jit(solution)/shard_map/all_to_all | solution.py:25
  33.0 0.1 all_to_all.59
  33.1 3.3 %all_gather.7 = bf16[192,1,1024]{2,0,1:T(8,128)(2,1)S(1)} all-gather(bf16[96,1,1024]{2,0,1:T(8,128)(2,1)S(1)} %all_to_all.59), channel_id=1, replica_groups=mesh['expert'=16,'pair'=2] {'pair'}, dimensions={0}, use_global_device_ids=true | all-gather | bytes 589824 | tf_op jit(solution)/shard_map/all_gather | solution.py:28
  36.4 4.1 %all-to-all-done = bf16[6,16,1024]{2,0,1:T(8,128)(2,1)S(1)} async-done(((bf16[6,16,1024]{2,0,1:T(8,128)(2,1)}), bf16[6,16,1024]{2,0,1:T(8,128)(2,1)S(1)}, u32[]{:S(2)}, u32[]{:S(2)}) %all-to-all-start) | async-done | bytes 196640 | tf_op jit(solution)/shard_map/all_to_all | solution.py:25
  40.5 0.1 all_to_all.55
  40.6 5.0 %all_gather.6 = bf16[192,1,1024]{2,0,1:T(8,128)(2,1)S(1)} all-gather(bf16[96,1,1024]{2,0,1:T(8,128)(2,1)S(1)} %all_to_all.55), channel_id=1, replica_groups=mesh['expert'=16,'pair'=2] {'pair'}, dimensions={0}, use_global_device_ids=true | all-gather | bytes 589824 | tf_op jit(solution)/shard_map/all_gather | solution.py:29
  45.6 3.4 %fusion.6 = f32[192,2048]{1,0:T(8,128)S(1)} fusion(bf16[1,1024,2048]{2,1,0:T(8,128)(2,1)} %param.7, bf16[192,1,1024]{2,0,1:T(8,128)(2,1)S(1)} %all_gather.7), kind=kOutput, calls=%fused_computation.7 | convolution fusion | flops 805306368 | bytes 6160384 | tf_op jit(solution)/shard_map/dot_general | solution.py:35
  49.0 0.2 copy-done.8
  49.2 2.2 fusion.18
  51.4 0.9 copy-done.3
  52.2 2.4 %fusion.4 = f32[192,1024]{1,0:T(8,128)} fusion(bf16[192,2048]{1,0:T(8,128)(2,1)S(1)} %fusion.18, bf16[1,1024,2048]{2,1,0:T(8,128)(2,1)S(1)} %copy-done.1), kind=kOutput, calls=%fused_computation.5 | convolution fusion | flops 805306368 | bytes 5767168 | tf_op jit(solution)/shard_map/dot_general | solution.py:43
  54.7 4.8 %fusion.8 = f32[192,1024]{1,0:T(8,128)} fusion(bf16[1,2048,1024]{2,1,0:T(8,128)(2,1)} %param.8, f32[192,2048]{1,0:T(8,128)} %copy-done.2), kind=kOutput, calls=%fused_computation.9 | convolution fusion | flops 808845312 | bytes 6553600 | tf_op jit(solution)/shard_map/dot_general | solution.py:37
  59.5 4.8 %convert_bitcast_fusion = bf16[1,2048,1024]{2,1,0:T(8,128)(2,1)} fusion(bf16[192,1,1024]{2,0,1:T(8,128)(2,1)S(1)} %copy-done.5, f32[192,2048]{1,0:T(8,128)} %copy-done.2), kind=kOutput, calls=%fused_computation.13 | convolution fusion | flops 810942464 | bytes 6160384 | tf_op jit(solution)/shard_map/dot_general | solution.py:49
  64.4 1.0 convert_bitcast_fusion.3
  65.4 0.5 broadcast.41
  65.9 0.7 reduce.2
  66.6 0.8 reshape.26
  67.4 3.5 %all-to-all-start.2 = ((bf16[16,2,3072]{2,1,0:T(2,128)(2,1)}), bf16[16,2,3072]{2,1,0:T(2,128)(2,1)S(1)}, u32[]{:S(2)}, u32[]{:S(2)}) async-start(bf16[16,2,3072]{2,1,0:T(2,128)(2,1)} %reshape.26), calls=%async_computation.3 | async-start | bytes 393216 | tf_op jit(solution)/shard_map/all_to_all | solution.py:60
  71.0 4.5 %convert_bitcast_fusion.1 = bf16[1,1024,2048]{2,1,0:T(8,128)(2,1)} fusion(bf16[192,2048]{1,0:T(8,128)(2,1)} %copy-done.3, bf16[192,1,1024]{2,0,1:T(8,128)(2,1)S(1)} %all_gather.7), kind=kOutput, calls=%fused_computation.14 | convolution fusion | flops 807403520 | bytes 5373952 | tf_op jit(solution)/shard_map/dot_general | solution.py:46
  75.4 1.0 convert_bitcast_fusion.2
  76.5 0.7 reduce.3
  77.2 0.8 reshape.28
  78.0 0.5 all-to-all-done.2
  78.5 5.8 %all-to-all-start.3 = ((bf16[16,2,3072]{2,1,0:T(2,128)(2,1)}), bf16[16,2,3072]{2,1,0:T(2,128)(2,1)S(1)}, u32[]{:S(2)}, u32[]{:S(2)}) async-start(bf16[16,2,3072]{2,1,0:T(2,128)(2,1)} %reshape.28), calls=%async_computation.5 | async-start | bytes 393216 | tf_op jit(solution)/shard_map/all_to_all | solution.py:59
  84.3 0.2 all-reduce.2.cloned.1.call-start
  84.5 0.1 reshape.27
  84.7 1.1 reduce
  85.9 0.7 convolution_bitcast_fusion
  86.6 3.5 %fusion.37 = f32[6,196,1024]{2,1,0:T(8,128)} fusion(bf16[16,6,1,1024]{3,1,0,2:T(8,128)(2,1)S(1)} %all_to_all.61, f32[6,16]{1,0:T(8,128)S(1)} %get-tuple-element.4, f32[6,196,16]{1,2,0:T(8,128)S(1)} %fusion.49), kind=kOutput, calls=%fused_computation.46 | convolution fusion | flops 38591908 | bytes 5089152 | tf_op jit(solution)/shard_map/nme,ned->nmd/dot_general | solution.py:68
  90.1 1.2 all-to-all-done.3
  91.3 0.1 reshape.29
  91.5 1.1 reduce.1
  92.7 2.4 %convolution_bitcast_fusion.1 = f32[6,196,16]{1,2,0:T(8,128)S(1)} fusion(bf16[6,196,1024]{2,1,0:T(8,128)(2,1)} %param.9, bf16[16,6,1,1024]{3,1,0,2:T(8,128)(2,1)S(1)} %all_to_all.65), kind=kOutput, calls=%fused_computation.36 | convolution fusion | flops 38535168 | bytes 2680320 | tf_op jit(solution)/shard_map/nmd,ned->nme/dot_general | solution.py:62
  95.1 0.3 fusion.26
  95.4 1.3 convolution_bitcast_fusion.2
  96.8 5.0 %add_convert_fusion = bf16[6,196,1024]{2,1,0:T(8,128)(2,1)} fusion(f32[6,196,1024]{2,1,0:T(8,128)} %fusion.37, f32[6,196,16]{1,2,0:T(8,128)S(1)} %fusion.26, f32[6,196,16]{1,2,0:T(8,128)S(1)} %convolution_bitcast_fusion, bf16[1024,16]{0,1:T(8,128)(2,1)S(1)} %copy-done.6, f32[6,196,16]{1,2,0:T(8,128)S(1)} %get-tuple-element.5, f32[6,16]{1,0:T(8,128)S(1)} %get-tuple-element.4), kind=kOutput, calls=%fused_computation.4 | convolution fusion | flops 41075620 | bytes 7484288 | tf_op jit(solution)/shard_map/dot_general | solution.py:71
  101.7 116.9 %all-reduce.2.cloned.1.call-done = f32[1024,16]{0,1:T(8,128)} async-done(((f32[1024,16]{0,1:T(8,128)}), f32[1024,16]{0,1:T(8,128)}) %all-reduce.2.cloned.1.call-update) | async-done | bytes 65552 | tf_op jit(solution)/shard_map/psum | solution.py:80
  218.6 1.5 copy.38
  (24 shorter events, 0.3 us)
Async XLA Ops:
  7.2 1.7 copy-start
  12.8 15.4 %all-to-all-start.1 = ((bf16[6,16,1024]{2,0,1:T(8,128)(2,1)}), bf16[6,16,1024]{2,0,1:T(8,128)(2,1)S(1)}, u32[]{:S(2)}, u32[]{:S(2)}) async-start(bf16[6,16,1024]{2,0,1:T(8,128)(2,1)} %copy.16), calls=%async_computation.1 | async-start | bytes 524288 | tf_op jit(solution)/shard_map/all_to_all | solution.py:24
  28.2 12.3 %all-to-all-start = ((bf16[6,16,1024]{2,0,1:T(8,128)(2,1)}), bf16[6,16,1024]{2,0,1:T(8,128)(2,1)S(1)}, u32[]{:S(2)}, u32[]{:S(2)}) async-start(bf16[6,16,1024]{2,0,1:T(8,128)(2,1)} %copy.15), calls=%async_computation | async-start | bytes 524288 | tf_op jit(solution)/shard_map/all_to_all | solution.py:25
  33.0 31.4 %reduce-scatter.3.cloned.1.call-start = ((), (), s32[]{:S(2)}) async-start(), calls=%async_computation.6 | async-start | bytes 1179648 | tf_op jit(solution)/shard_map/reduce_scatter | solution.py:54
  45.6 3.4 %copy-start.4 = (bf16[192,1,1024]{2,0,1:T(8,128)(2,1)}, bf16[192,1,1024]{2,0,1:T(8,128)(2,1)S(1)}, u32[]{:S(2)}) copy-start(bf16[192,1,1024]{2,0,1:T(8,128)(2,1)S(1)} %all_gather.6) | copy-start | bytes 1179652
  45.6 3.6 %copy-start.8 = (bf16[1,2048,1024]{2,1,0:T(8,128)(2,1)S(1)}, bf16[1,2048,1024]{2,1,0:T(8,128)(2,1)}, u32[]{:S(2)}) copy-start(bf16[1,2048,1024]{2,1,0:T(8,128)(2,1)} %param.8) | copy-start | bytes 12582916
  49.2 2.2 copy-start.2
  49.2 3.1 %copy-start.1 = (bf16[1,1024,2048]{2,1,0:T(8,128)(2,1)S(1)}, bf16[1,1024,2048]{2,1,0:T(8,128)(2,1)}, u32[]{:S(2)}) copy-start(bf16[1,1024,2048]{2,1,0:T(8,128)(2,1)} %param.7) | copy-start | bytes 12582916
  51.4 0.9 copy-start.3
  54.7 4.9 %copy-start.5 = (bf16[192,1,1024]{2,0,1:T(8,128)(2,1)S(1)}, bf16[192,1,1024]{2,0,1:T(8,128)(2,1)}, u32[]{:S(2)}) copy-start(bf16[192,1,1024]{2,0,1:T(8,128)(2,1)} %copy-done.4) | copy-start | bytes 1179652
  54.7 20.7 %reduce-scatter.5.cloned.1.call-start = ((), (), s32[]{:S(2)}) async-start(), calls=%async_computation.7 | async-start | bytes 1179648 | tf_op jit(solution)/shard_map/reduce_scatter | solution.py:53
  67.4 11.0 %all-to-all-start.2 = ((bf16[16,2,3072]{2,1,0:T(2,128)(2,1)}), bf16[16,2,3072]{2,1,0:T(2,128)(2,1)S(1)}, u32[]{:S(2)}, u32[]{:S(2)}) async-start(bf16[16,2,3072]{2,1,0:T(2,128)(2,1)} %reshape.26), calls=%async_computation.3 | async-start | bytes 393216 | tf_op jit(solution)/shard_map/all_to_all | solution.py:60
  78.5 12.8 %all-to-all-start.3 = ((bf16[16,2,3072]{2,1,0:T(2,128)(2,1)}), bf16[16,2,3072]{2,1,0:T(2,128)(2,1)S(1)}, u32[]{:S(2)}, u32[]{:S(2)}) async-start(bf16[16,2,3072]{2,1,0:T(2,128)(2,1)} %reshape.28), calls=%async_computation.5 | async-start | bytes 393216 | tf_op jit(solution)/shard_map/all_to_all | solution.py:59
  84.3 134.3 %all-reduce.2.cloned.1.call-start = ((), (), s32[]{:S(2)}) async-start(), calls=%async_computation.8 | async-start | bytes 131072 | tf_op jit(solution)/shard_map/psum | solution.py:80
  92.6 2.5 %copy-start.7 = (f32[6,196,16]{1,2,0:T(8,128)S(1)}, f32[6,196,16]{1,2,0:T(8,128)}, u32[]{:S(2)}) copy-start(f32[6,196,16]{1,2,0:T(8,128)} %get-tuple-element.7) | copy-start | bytes 225796
  95.4 1.4 copy-start.6
Sparse Core Ops, SparseCore 0:
  54.8 6.1 reduce-scatter.2
  63.2 9.2 reduce-scatter.4
  96.9 121.6 all-reduce.1
where the time goes:
time: 228 us; the launch traced here: 227 us
  waiting for transfers between devices  127 us (56%)
  matrix products  39.2 us (17%)
  starting transfers between devices  21.9 us (10%)
  between operations  13.9 us (6%)
  local copies, waits for them, and re-layouts  8.63 us (4%)
  blocking collectives  8.31 us (4%)
  other arithmetic  7.7 us (3%)
    psum x1, waiting for transfers between devices, per_device(): router_grad = lax.psum(router_part, ('expert', 'pair'))  117 us
    all_to_all x1, starting transfers between devices, per_device(): lax.all_to_all(slot_values, 'expert', split_axis=1, concat_axis=0, tiled=...  7.4 us
    unnamed x23, local copies, waits for them, and re-layouts  6.18 us
    all_to_all x1, starting transfers between devices, per_device(): lax.all_to_all(out_rows, 'expert', split_axis=0, concat_axis=1, tiled=True)  5.83 us
    all_gather x1, blocking collectives, per_device(): lax.all_gather(moved[1], 'pair', axis=0, tiled=True)  5.04 us
    dot_general x1, matrix products, per_device(): lax.dot_general(flat_logit, router, (((1,), (1,)), ((), ())), preferred_e...  4.95 us
    dot_general x1, matrix products, per_device(): lax.dot_general(activated, cot_rows, (((0,), (0,)), ((), ())), preferred_...  4.83 us
    all_to_all x1, starting transfers between devices, per_device(): lax.all_to_all(slot_cot, 'expert', split_axis=1, concat_axis=0, tiled=True)  4.79 us
  transfers between devices with their start and end apart: 7, of which 5 were waited for; matrix products, arithmetic and copies ran while one was open for 15% of the time, Pallas kernels for 0%

commit v1 on v0

--- a/solution.py
+++ b/solution.py
@@ -77,7 +77,7 @@
     router_part = lax.dot_general(
         flat_tokens, flat_logit, (((0,), (0,)), ((), ())), preferred_element_type=jnp.float32
     )
-    router_grad = lax.psum(router_part, ("expert", "pair"))
+    router_grad = jnp.sum(lax.all_gather(router_part, ("expert", "pair")), axis=0)
     return (
         tokens_grad,
         grad_in.astype(jnp.bfloat16)[None],

time: 228 us -> 170 us (0.75)
  waiting for transfers between devices: 127 us -> 55.1 us
  local copies, waits for them, and re-layouts: 8.63 us -> 14.4 us
  other arithmetic: 7.7 us -> 12.5 us
  starting transfers between devices: 21.9 us -> 24.9 us
    psum x1 -> x0, waiting for transfers between devices: 117 us -> none  [per_device(): router_grad = lax.psum(router_part, ('expert', 'pair'))]
    all_gather x0 -> x1, waiting for transfers between devices: none -> 39.8 us  [per_device(): lax.all_gather(router_part, ('expert', 'pair'))]
    unnamed x23 -> x29, local copies, waits for them, and re-layouts: 6.18 us -> 10.3 us
    all_to_all x1, starting transfers between devices: 3.52 us -> 6.62 us  [per_device(): lax.all_to_all(grad_rows, 'expert', split_axis=0, concat_axis=1, tiled=True)]
    reduce_scatter x1, waiting for transfers between devices: 0.01 us -> 2.43 us  [per_device(): lax.psum_scatter(out_partial, 'pair', scatter_dimension=0, tiled=True)]
  transfers between devices with their start and end apart: 7 -> 7, of which waited for: 5 -> 7; matrix products, arithmetic and copies ran while one was open for 15% -> 22% of each run, Pallas kernels for 0% -> 0%
where the time goes in v1:
time: 170 us; the launch traced here: 169 us
  waiting for transfers between devices  55.1 us (32%)
  matrix products  39.4 us (23%)
  starting transfers between devices  24.9 us (15%)
  local copies, waits for them, and re-layouts  14.4 us (8%)
  between operations  13.9 us (8%)
  other arithmetic  12.5 us (7%)
  blocking collectives  8.51 us (5%)
    all_gather x1, waiting for transfers between devices, per_device(): lax.all_gather(router_part, ('expert', 'pair'))  39.8 us
    unnamed x29, local copies, waits for them, and re-layouts  10.3 us
    all_to_all x1, starting transfers between devices, per_device(): lax.all_to_all(slot_values, 'expert', split_axis=1, concat_axis=0, tiled=...  7.4 us
    all_to_all x1, starting transfers between devices, per_device(): lax.all_to_all(grad_rows, 'expert', split_axis=0, concat_axis=1, tiled=True)  6.62 us
    all_to_all x1, starting transfers between devices, per_device(): lax.all_to_all(out_rows, 'expert', split_axis=0, concat_axis=1, tiled=True)  5.76 us
    all_gather x1, blocking collectives, per_device(): lax.all_gather(moved[1], 'pair', axis=0, tiled=True)  5.04 us
    dot_general x1, matrix products, per_device(): lax.dot_general(flat_logit, router, (((1,), (1,)), ((), ())), preferred_e...  4.95 us
    all_to_all x1, starting transfers between devices, per_device(): lax.all_to_all(slot_cot, 'expert', split_axis=1, concat_axis=0, tiled=True)  4.79 us
  transfers between devices with their start and end apart: 7, of which 7 were waited for; matrix products, arithmetic and copies ran while one was open for 22% of the time, Pallas kernels for 0%

profile of v1, /device:TPU:1, one launch (start us, length us, event | category | flops | bytes accessed | tf_op | source)
XLA Modules:
  0.0 168.7 jit_solution(11423440730896065451)
XLA Ops:
  7.2 1.7 copy-done
  8.9 1.5 fusion.49
  10.4 0.8 fusion.55
  11.1 0.5 convolution_convert_fusion
  11.6 0.8 copy.16
  12.5 7.4 %all-to-all-start.1 = ((bf16[6,16,1024]{2,0,1:T(8,128)(2,1)}), bf16[6,16,1024]{2,0,1:T(8,128)(2,1)S(1)}, u32[]{:S(2)}, u32[]{:S(2)}) async-start(bf16[6,16,1024]{2,0,1:T(8,128)(2,1)} %copy.16), calls=%async_computation.1 | async-start | bytes 524288 | tf_op jit(solution)/shard_map/all_to_all | solution.py:24
  19.9 0.7 fusion.56
  20.6 2.2 %convolution_convert_fusion.1 = bf16[6,16,1024]{2,1,0:T(8,128)(2,1)S(1)} fusion(bf16[6,196,1024]{2,1,0:T(8,128)(2,1)} %param.9, f32[6,196]{1,0:T(8,128)S(1)} %get-tuple-element.6, f32[6,196,16]{1,2,0:T(8,128)S(1)} %fusion.49), kind=kOutput, calls=%fused_computation.27 | convolution fusion | flops 38691112 | bytes 2685024 | tf_op jit(solution)/shard_map/nme,nmd->ned/dot_general | solution.py:20
  22.8 0.8 copy.15
  23.6 4.3 %all-to-all-done.1 = bf16[6,16,1024]{2,0,1:T(8,128)(2,1)S(1)} async-done(((bf16[6,16,1024]{2,0,1:T(8,128)(2,1)}), bf16[6,16,1024]{2,0,1:T(8,128)(2,1)S(1)}, u32[]{:S(2)}, u32[]{:S(2)}) %all-to-all-start.1) | async-done | bytes 196640 | tf_op jit(solution)/shard_map/all_to_all | solution.py:24
  27.9 4.8 %all-to-all-start = ((bf16[6,16,1024]{2,0,1:T(8,128)(2,1)}), bf16[6,16,1024]{2,0,1:T(8,128)(2,1)S(1)}, u32[]{:S(2)}, u32[]{:S(2)}) async-start(bf16[6,16,1024]{2,0,1:T(8,128)(2,1)} %copy.15), calls=%async_computation | async-start | bytes 524288 | tf_op jit(solution)/shard_map/all_to_all | solution.py:25
  32.8 0.7 all_to_all.59
  33.5 3.5 %all_gather.13 = bf16[192,1,1024]{2,0,1:T(8,128)(2,1)S(1)} all-gather(bf16[96,1,1024]{2,0,1:T(8,128)(2,1)} %all_to_all.59), channel_id=1, replica_groups=mesh['expert'=16,'pair'=2] {'pair'}, dimensions={0}, use_global_device_ids=true | all-gather | bytes 589824 | tf_op jit(solution)/shard_map/all_gather | solution.py:28
  37.0 3.2 %all-to-all-done = bf16[6,16,1024]{2,0,1:T(8,128)(2,1)S(1)} async-done(((bf16[6,16,1024]{2,0,1:T(8,128)(2,1)}), bf16[6,16,1024]{2,0,1:T(8,128)(2,1)S(1)}, u32[]{:S(2)}, u32[]{:S(2)}) %all-to-all-start) | async-done | bytes 196640 | tf_op jit(solution)/shard_map/all_to_all | solution.py:25
  40.3 5.0 %all_gather.12 = bf16[192,1,1024]{2,0,1:T(8,128)(2,1)S(1)} all-gather(bf16[96,1,1024]{2,0,1:T(8,128)(2,1)S(1)} %all_to_all.55), channel_id=1, replica_groups=mesh['expert'=16,'pair'=2] {'pair'}, dimensions={0}, use_global_device_ids=true | all-gather | bytes 589824 | tf_op jit(solution)/shard_map/all_gather | solution.py:29
  45.3 3.4 %fusion.6 = f32[192,2048]{1,0:T(8,128)S(1)} fusion(bf16[1,1024,2048]{2,1,0:T(8,128)(2,1)} %param.7, bf16[192,1,1024]{2,0,1:T(8,128)(2,1)S(1)} %all_gather.13), kind=kOutput, calls=%fused_computation.7 | convolution fusion | flops 805306368 | bytes 6160384 | tf_op jit(solution)/shard_map/dot_general | solution.py:35
  48.9 2.2 %fusion.18 = bf16[192,2048]{1,0:T(8,128)(2,1)S(1)} fusion(f32[192,2048]{1,0:T(8,128)S(1)} %fusion.6, bf16[1,2048,1024]{2,1,0:T(8,128)(2,1)S(1)} %copy-done.11, bf16[192,1,1024]{2,0,1:T(8,128)(2,1)S(1)} %all_gather.12), kind=kOutput, calls=%fused_computation.24 | convolution fusion | flops 813170688 | bytes 6946816 | tf_op jit(solution)/shard_map/dot_general | solution.py:38
  51.1 0.9 copy-done.4
  52.0 2.4 %fusion.4 = f32[192,1024]{1,0:T(8,128)} fusion(bf16[192,2048]{1,0:T(8,128)(2,1)S(1)} %fusion.18, bf16[1,1024,2048]{2,1,0:T(8,128)(2,1)S(1)} %copy-done.1), kind=kOutput, calls=%fused_computation.5 | convolution fusion | flops 805306368 | bytes 5767168 | tf_op jit(solution)/shard_map/dot_general | solution.py:43
  54.5 4.7 %fusion.8 = f32[192,1024]{1,0:T(8,128)} fusion(bf16[1,2048,1024]{2,1,0:T(8,128)(2,1)} %param.8, f32[192,2048]{1,0:T(8,128)} %copy-done.2), kind=kOutput, calls=%fused_computation.9 | convolution fusion | flops 808845312 | bytes 6553600 | tf_op jit(solution)/shard_map/dot_general | solution.py:37
  59.2 1.5 reduce-scatter.3.cloned.1.call-done
  60.7 1.0 convert_bitcast_fusion.3
  61.7 0.5 broadcast.41
  62.2 0.7 reduce.2
  63.0 0.8 reshape.27
  63.8 6.6 %all-to-all-start.2 = ((bf16[16,2,3072]{2,1,0:T(2,128)(2,1)}), bf16[16,2,3072]{2,1,0:T(2,128)(2,1)S(1)}, u32[]{:S(2)}, u32[]{:S(2)}) async-start(bf16[16,2,3072]{2,1,0:T(2,128)(2,1)} %reshape.27), calls=%async_computation.3 | async-start | bytes 393216 | tf_op jit(solution)/shard_map/all_to_all | solution.py:60
  70.4 2.4 %reduce-scatter.5.cloned.1.call-done = f32[96,1024]{1,0:T(8,128)} async-done(((f32[192,1024]{1,0:T(8,128)}), f32[96,1024]{1,0:T(8,128)}) %reduce-scatter.5.cloned.1.call-update) | async-done | bytes 393232 | tf_op jit(solution)/shard_map/reduce_scatter | solution.py:53
  72.8 1.7 %convert_bitcast_fusion.2 = bf16[96,1,1024]{2,0,1:T(8,128)(2,1)} fusion(f32[96,1024]{1,0:T(8,128)} %reduce-scatter.5.cloned.1.call-done), kind=kLoop, calls=%fused_computation.50 | loop fusion | flops 98304 | bytes 589824 | tf_op jit(solution)/shard_map/broadcast_in_dim | solution.py:56
  74.5 1.6 reduce.3
  76.2 0.8 reshape.29
  77.0 0.9 all-to-all-done.2
  77.9 5.8 %all-to-all-start.3 = ((bf16[16,2,3072]{2,1,0:T(2,128)(2,1)}), bf16[16,2,3072]{2,1,0:T(2,128)(2,1)}, u32[]{:S(2)}, u32[]{:S(2)}) async-start(bf16[16,2,3072]{2,1,0:T(2,128)(2,1)} %reshape.29), calls=%async_computation.5 | async-start | bytes 393216 | tf_op jit(solution)/shard_map/all_to_all | solution.py:59
  83.9 0.9 reshape.28
  84.8 2.1 %reduce = bf16[96,1024]{1,0:T(8,128)(2,1)S(1)} reduce(bf16[96,1,1024]{2,1,0:T(2,128)(2,1)} %reshape.28, bf16[]{:T(256)} %constant.22), dimensions={1}, to_apply=%all_to_all.60.reduce_sub_computation | reduce | bytes 393218 | tf_op jit(solution)/shard_map/all_to_all | solution.py:60
  86.9 1.4 convolution_bitcast_fusion
  88.3 2.8 %all-to-all-done.3 = bf16[16,2,3072]{2,1,0:T(2,128)(2,1)} async-done(((bf16[16,2,3072]{2,1,0:T(2,128)(2,1)}), bf16[16,2,3072]{2,1,0:T(2,128)(2,1)}, u32[]{:S(2)}, u32[]{:S(2)}) %all-to-all-start.3) | async-done | bytes 196640 | tf_op jit(solution)/shard_map/all_to_all | solution.py:59
  91.2 2.2 %reshape.30 = bf16[96,1,1024]{2,1,0:T(2,128)(2,1)} reshape(bf16[16,2,3072]{2,1,0:T(2,128)(2,1)} %all-to-all-done.3) | data formatting | bytes 393216
  93.4 2.8 %reduce.1 = bf16[96,1024]{1,0:T(8,128)(2,1)} reduce(bf16[96,1,1024]{2,1,0:T(2,128)(2,1)} %reshape.30, bf16[]{:T(256)} %constant.22), dimensions={1}, to_apply=%all_to_all.64.reduce_sub_computation | reduce | bytes 393218 | tf_op jit(solution)/shard_map/all_to_all | solution.py:59
  96.2 1.0 all_to_all.65
  97.2 2.5 %convolution_bitcast_fusion.1 = f32[6,196,16]{1,2,0:T(8,128)S(1)} fusion(bf16[6,196,1024]{2,1,0:T(8,128)(2,1)} %param.9, bf16[16,6,1,1024]{3,1,0,2:T(8,128)(2,1)S(1)} %all_to_all.65), kind=kOutput, calls=%fused_computation.37 | convolution fusion | flops 38535168 | bytes 2680320 | tf_op jit(solution)/shard_map/nmd,ned->nme/dot_general | solution.py:62
  100.0 2.4 %convolution_bitcast_fusion.2 = f32[1024,16]{0,1:T(8,128)} fusion(bf16[6,196,1024]{2,1,0:T(8,128)(2,1)S(1)} %copy-done, f32[6,196,16]{1,2,0:T(8,128)S(1)} %fusion.26, f32[6,196,16]{1,2,0:T(8,128)} %convolution_bitcast_fusion, f32[6,196,16]{1,2,0:T(8,128)} %get-tuple-element.5, f32[6,16]{1,0:T(8,128)S(1)} %get-tuple-element.4), kind=kOutput, calls=%fused_computation.40 | convolution fusion | flops 38667172 | bytes 2700160 | tf_op jit(solution)/shard_map/dot_general | solution.py:77
  102.3 4.6 %convert_bitcast_fusion.1 = bf16[1,1024,2048]{2,1,0:T(8,128)(2,1)} fusion(bf16[192,2048]{1,0:T(8,128)(2,1)} %copy-done.4, bf16[192,1,1024]{2,0,1:T(8,128)(2,1)S(1)} %all_gather.13), kind=kOutput, calls=%fused_computation.14 | convolution fusion | flops 807403520 | bytes 5373952 | tf_op jit(solution)/shard_map/dot_general | solution.py:46
  106.9 3.4 %convert_bitcast_fusion = bf16[1,2048,1024]{2,1,0:T(8,128)(2,1)} fusion(bf16[192,1,1024]{2,0,1:T(8,128)(2,1)S(1)} %copy-done.8, f32[192,2048]{1,0:T(8,128)S(1)} %copy-done.3), kind=kOutput, calls=%fused_computation.13 | convolution fusion | flops 810942464 | bytes 6160384 | tf_op jit(solution)/shard_map/dot_general | solution.py:49
  110.3 3.4 %fusion.37 = f32[6,196,1024]{2,1,0:T(8,128)} fusion(bf16[16,6,1,1024]{3,1,0,2:T(8,128)(2,1)S(1)} %all_to_all.61, f32[6,16]{1,0:T(8,128)S(1)} %get-tuple-element.4, f32[6,196,16]{1,2,0:T(8,128)S(1)} %fusion.49), kind=kOutput, calls=%fused_computation.47 | convolution fusion | flops 38591908 | bytes 5089152 | tf_op jit(solution)/shard_map/nme,ned->nmd/dot_general | solution.py:68
  113.7 4.9 %add_convert_fusion = bf16[6,196,1024]{2,1,0:T(8,128)(2,1)} fusion(f32[6,196,1024]{2,1,0:T(8,128)} %fusion.37, f32[6,196,16]{1,2,0:T(8,128)S(1)} %fusion.26, f32[6,196,16]{1,2,0:T(8,128)S(1)} %copy-done.5, bf16[1024,16]{0,1:T(8,128)(2,1)S(1)} %copy-done.9, f32[6,196,16]{1,2,0:T(8,128)S(1)} %copy-done.6, f32[6,16]{1,0:T(8,128)S(1)} %get-tuple-element.4), kind=kOutput, calls=%fused_computation.4 | convolution fusion | flops 41075620 | bytes 7484288 | tf_op jit(solution)/shard_map/dot_general | solution.py:71
  118.7 39.8 %all-gather.3.cloned.1.call-done = f32[32768,16]{0,1:T(8,128)} async-done(((f32[1024,16]{0,1:T(8,128)}), f32[32768,16]{0,1:T(8,128)}) %all-gather.3.cloned.1.call-update) | async-done | bytes 2097168 | tf_op jit(solution)/shard_map/all_gather | solution.py:80
  158.5 2.8 %copy.23 = f32[2,8,32,1024]{3,2,1,0:T(8,128)S(1)} copy(f32[2,8,32,1024]{3,1,2,0:T(8,128)} %bitcast.83) | data formatting | bytes 4194304
  161.3 0.8 bitcast_reduce_fusion
  (31 shorter events, 1.1 us)
Async XLA Ops:
  7.2 1.7 %copy-start = (bf16[6,196,1024]{2,1,0:T(8,128)(2,1)S(1)}, bf16[6,196,1024]{2,1,0:T(8,128)(2,1)}, u32[]{:S(2)}) copy-start(bf16[6,196,1024]{2,1,0:T(8,128)(2,1)} %param.5) | copy-start | bytes 7225348
  12.5 15.4 %all-to-all-start.1 = ((bf16[6,16,1024]{2,0,1:T(8,128)(2,1)}), bf16[6,16,1024]{2,0,1:T(8,128)(2,1)S(1)}, u32[]{:S(2)}, u32[]{:S(2)}) async-start(bf16[6,16,1024]{2,0,1:T(8,128)(2,1)} %copy.16), calls=%async_computation.1 | async-start | bytes 524288 | tf_op jit(solution)/shard_map/all_to_all | solution.py:24
  27.9 12.3 %all-to-all-start = ((bf16[6,16,1024]{2,0,1:T(8,128)(2,1)}), bf16[6,16,1024]{2,0,1:T(8,128)(2,1)S(1)}, u32[]{:S(2)}, u32[]{:S(2)}) async-start(bf16[6,16,1024]{2,0,1:T(8,128)(2,1)} %copy.15), calls=%async_computation | async-start | bytes 524288 | tf_op jit(solution)/shard_map/all_to_all | solution.py:25
  32.7 28.0 %reduce-scatter.3.cloned.1.call-start = ((), (), s32[]{:S(2)}) async-start(), calls=%async_computation.6 | async-start | bytes 1179648 | tf_op jit(solution)/shard_map/reduce_scatter | solution.py:54
  45.3 3.4 %copy-start.7 = (bf16[192,1,1024]{2,0,1:T(8,128)(2,1)}, bf16[192,1,1024]{2,0,1:T(8,128)(2,1)S(1)}, u32[]{:S(2)}) copy-start(bf16[192,1,1024]{2,0,1:T(8,128)(2,1)S(1)} %all_gather.12) | copy-start | bytes 1179652
  45.3 3.6 %copy-start.11 = (bf16[1,2048,1024]{2,1,0:T(8,128)(2,1)S(1)}, bf16[1,2048,1024]{2,1,0:T(8,128)(2,1)}, u32[]{:S(2)}) copy-start(bf16[1,2048,1024]{2,1,0:T(8,128)(2,1)} %param.8) | copy-start | bytes 12582916
  48.9 2.2 %copy-start.2 = (f32[192,2048]{1,0:T(8,128)}, f32[192,2048]{1,0:T(8,128)S(1)}, u32[]{:S(2)}) copy-start(f32[192,2048]{1,0:T(8,128)S(1)} %fusion.6) | copy-start | bytes 4718596
  48.9 3.1 %copy-start.1 = (bf16[1,1024,2048]{2,1,0:T(8,128)(2,1)S(1)}, bf16[1,1024,2048]{2,1,0:T(8,128)(2,1)}, u32[]{:S(2)}) copy-start(bf16[1,1024,2048]{2,1,0:T(8,128)(2,1)} %param.7) | copy-start | bytes 12582916
  51.1 0.9 copy-start.4
  54.4 18.4 %reduce-scatter.5.cloned.1.call-start = ((), (), s32[]{:S(2)}) async-start(), calls=%async_computation.7 | async-start | bytes 1179648 | tf_op jit(solution)/shard_map/reduce_scatter | solution.py:53
  63.8 14.1 %all-to-all-start.2 = ((bf16[16,2,3072]{2,1,0:T(2,128)(2,1)}), bf16[16,2,3072]{2,1,0:T(2,128)(2,1)S(1)}, u32[]{:S(2)}, u32[]{:S(2)}) async-start(bf16[16,2,3072]{2,1,0:T(2,128)(2,1)} %reshape.27), calls=%async_computation.3 | async-start | bytes 393216 | tf_op jit(solution)/shard_map/all_to_all | solution.py:60
  77.9 13.3 %all-to-all-start.3 = ((bf16[16,2,3072]{2,1,0:T(2,128)(2,1)}), bf16[16,2,3072]{2,1,0:T(2,128)(2,1)}, u32[]{:S(2)}, u32[]{:S(2)}) async-start(bf16[16,2,3072]{2,1,0:T(2,128)(2,1)} %reshape.29), calls=%async_computation.5 | async-start | bytes 393216 | tf_op jit(solution)/shard_map/all_to_all | solution.py:59
  83.7 74.9 %all-gather.3.cloned.1.call-start = ((), (), s32[]{:S(2)}) async-start(), calls=%async_computation.8 | async-start | bytes 2162688 | tf_op jit(solution)/shard_map/all_gather | solution.py:80
  97.1 2.5 %copy-start.10 = (f32[6,196,16]{1,2,0:T(8,128)S(1)}, f32[6,196,16]{1,2,0:T(8,128)}, u32[]{:S(2)}) copy-start(f32[6,196,16]{1,2,0:T(8,128)} %get-tuple-element.7) | copy-start | bytes 225796
  102.3 4.6 %copy-start.3 = (f32[192,2048]{1,0:T(8,128)S(1)}, f32[192,2048]{1,0:T(8,128)}, u32[]{:S(2)}) copy-start(f32[192,2048]{1,0:T(8,128)} %copy-done.2) | copy-start | bytes 4718596
  102.3 4.6 %copy-start.8 = (bf16[192,1,1024]{2,0,1:T(8,128)(2,1)S(1)}, bf16[192,1,1024]{2,0,1:T(8,128)(2,1)}, u32[]{:S(2)}) copy-start(bf16[192,1,1024]{2,0,1:T(8,128)(2,1)} %copy-done.7) | copy-start | bytes 1179652
  110.3 3.4 %copy-start.5 = (f32[6,196,16]{1,2,0:T(8,128)S(1)}, f32[6,196,16]{1,2,0:T(8,128)}, u32[]{:S(2)}) copy-start(f32[6,196,16]{1,2,0:T(8,128)} %convolution_bitcast_fusion) | copy-start | bytes 225796
  110.3 3.4 %copy-start.6 = (f32[6,196,16]{1,2,0:T(8,128)S(1)}, f32[6,196,16]{1,2,0:T(8,128)}, u32[]{:S(2)}) copy-start(f32[6,196,16]{1,2,0:T(8,128)} %get-tuple-element.5) | copy-start | bytes 225796
  110.3 3.4 %copy-start.9 = (bf16[1024,16]{0,1:T(8,128)(2,1)S(1)}, bf16[1024,16]{0,1:T(8,128)(2,1)}, u32[]{:S(2)}) copy-start(bf16[1024,16]{0,1:T(8,128)(2,1)} %param.6) | copy-start | bytes 98308
Sparse Core Ops, SparseCore 0:
  54.5 6.1 reduce-scatter.2
  63.5 9.2 reduce-scatter.4
  102.4 56.0 all-gather.2
